TPU v7x, 256 devices: a whole 4x4x8 slice. The times are simulated.
256 devices in a mesh: dp: 8 (over x, y_lo), seq: 32 (over z, y_hi, core).
Axes of the slice: x: 4, y: 4 (y_hi: 2, y_lo: 2; y = y_hi * 2 + y_lo), z: 8, core: 2. Of those that a mesh axis runs over, the one named last changes fastest.
Arguments:
- x_fwd: bfloat16 [131072, 1024], P(('dp', 'seq')), parts along dimension 0, may hold values from -6 to 6
- x_rev: bfloat16 [131072, 1024], P(('dp', 'seq')), parts along dimension 0, may hold values from -6 to 6
- gain: bfloat16 [1024], replicated, may hold values from 0.099609375 to 1.8984375
- w_qkv: bfloat16 [1024, 3072], replicated
Outputs:
- y_fwd: bfloat16 [131072, 1024], P(('dp', 'seq')), parts along dimension 0
- y_rev: bfloat16 [131072, 1024], P(('dp', 'seq')), parts along dimension 0
There are 8 independent parts, one for each index of `dp`. A program takes and returns all parts, laid end to end along the dimension named above; an argument that names none is the same for every part. Nothing has to cross between parts.
All inputs are finite; a program needn't handle non-finite values.
Results may differ from a plain program's by a relative error of at most 0.012.
Values may be sent and summed in bfloat16 or wider, within the bound.
No kernel may reach another device: no remote copies, remote signals or barrier semaphores. Data moves between devices by JAX's collectives and lax.ppermute only.
A program may use at most 128 MiB of HBM per device.

v0:
```python
import jax
import jax.numpy as jnp
from jax import lax
from jax.sharding import PartitionSpec as P

HEADS = 16
WINDOW = 512


def extended_2(cells, sides, width):
    for axis, dim in sides:
        count = lax.axis_size(axis)
        ends = count - 1
        head = lax.slice_in_dim(cells, 0, width, axis=dim)
        tail = lax.slice_in_dim(cells, cells.shape[dim] - width, cells.shape[dim], axis=dim)
        cells = jnp.concatenate(
            [
                lax.ppermute(tail, axis, [(i, (i + 1) % count) for i in range(ends)]),
                cells,
                lax.ppermute(head, axis, [((i + 1) % count, i) for i in range(ends)]),
            ],
            axis=dim,
        )
    return cells


def attend(stacked, gain, w_qkv):
    rows = stacked.shape[1]
    width = stacked.shape[2]
    head_size = width // HEADS
    per_group = 2
    group_width = per_group * head_size
    span = rows + 2 * WINDOW
    scale = head_size ** (-0.5)
    xf = stacked.astype(jnp.float32)
    meansq = jnp.mean(xf * xf, axis=-1, keepdims=True)
    normed = (xf * lax.rsqrt(meansq + 1e-06) * gain.astype(jnp.float32)).astype(jnp.bfloat16)
    qkv = jnp.dot(normed.reshape(2 * rows, width), w_qkv, preferred_element_type=jnp.float32)
    qkv = qkv.astype(jnp.bfloat16).reshape(2, rows, 3 * width)
    query = qkv[:, :, :width]
    keyval = qkv[:, :, width:]
    extended = extended_2(keyval, (("seq", 1),), WINDOW)
    length = rows * lax.axis_size("seq")
    start = lax.axis_index("seq") * rows
    qpos = start + jnp.arange(rows, dtype=jnp.int32)
    kpos = start - WINDOW + jnp.arange(span, dtype=jnp.int32)
    inside = (
        (jnp.abs(qpos[:, None] - kpos[None, :]) <= WINDOW)
        & (kpos[None, :] >= 0)
        & (kpos[None, :] < length)
    )

    def group_heads(group):
        offset = group * group_width
        qgroup = lax.dynamic_slice_in_dim(query, offset, group_width, 2).reshape(
            2, rows, per_group, head_size
        )
        kgroup = lax.dynamic_slice_in_dim(extended, offset, group_width, 2).reshape(
            2, span, per_group, head_size
        )
        vgroup = lax.dynamic_slice_in_dim(extended, width + offset, group_width, 2).reshape(
            2, span, per_group, head_size
        )
        scores = (
            jnp.einsum("srhd,skhd->shrk", qgroup, kgroup, preferred_element_type=jnp.float32)
            * scale
        )
        scores = jnp.where(inside[None, None], scores, -1e30)
        top = jnp.max(scores, axis=-1, keepdims=True)
        probs = jnp.exp(scores - top)
        denom = jnp.sum(probs, axis=-1)
        weights = probs.astype(jnp.bfloat16)
        out = jnp.einsum("shrk,skhd->srhd", weights, vgroup, preferred_element_type=jnp.float32)
        out = out / jnp.transpose(denom, (0, 2, 1))[:, :, :, None]
        return out.reshape(2, rows, group_width).astype(jnp.bfloat16)

    grouped = lax.map(group_heads, jnp.arange(HEADS // per_group, dtype=jnp.int32))
    return jnp.transpose(grouped, (1, 2, 0, 3)).reshape(2, rows, width)


def split_pieces(block):
    count = lax.axis_size("seq")
    lead = block.shape[0]
    rows = block.shape[1]
    width = block.shape[2]
    return block.reshape(lead, rows, count, width // count)


def combine_outputs(attended, moved):
    partner = moved[:, ::-1, ::-1].astype(jnp.float32)
    near = attended.astype(jnp.float32)
    y_fwd = (near[0] + partner[1]).astype(jnp.bfloat16)
    y_rev = (near[1] + partner[0]).astype(jnp.bfloat16)
    return (y_fwd, y_rev)


def per_device(x_fwd, x_rev, gain, w_qkv):
    attended = attend(jnp.stack([x_fwd, x_rev]), gain, w_qkv)
    pieces = split_pieces(attended)
    spread = lax.all_to_all(pieces, "seq", split_axis=2, concat_axis=2, tiled=True)[:, :, ::-1]
    moved = lax.all_to_all(spread, "seq", split_axis=2, concat_axis=2, tiled=True).reshape(
        attended.shape
    )
    y_fwd, y_rev = combine_outputs(attended, moved)
    return (y_fwd, y_rev)


def solution(mesh):
    in_specs = (P(("dp", "seq"), None), P(("dp", "seq"), None), P(), P())
    out_specs = (P(("dp", "seq"), None), P(("dp", "seq"), None))
    return jax.shard_map(
        per_device, mesh=mesh, in_specs=in_specs, out_specs=out_specs, check_vma=False
    )
```

profile of v0, /device:TPU:25, one launch (start us, length us, event | category | flops | bytes accessed | tf_op | source)
XLA Modules:
  0.0 411.1 jit_solution(2662625279337310924)
XLA Ops:
  4.9 7.1 %convolution_convert_fusion = bf16[1024,3072]{1,0:T(8,128)(2,1)S(1)} fusion(bf16[1024,1024]{1,0:T(8,128)(2,1)S(1)} %fusion.22, bf16[1024,3072]{1,0:T(8,128)(2,1)S(1)} %bitcast.79), kind=kOutput, calls=%fused_computation.21 | convolution fusion | flops 6445596672 | bytes 14680064 | tf_op jit(solution)/shard_map/dot_general | solution.py:38
  17.0 6.3 %copy.24 = bf16[2,512,2048]{1,2,0:T(8,128)(2,1)} copy(bf16[2,512,2048]{2,1,0:T(8,128)(2,1)} %slice.32) | data formatting | bytes 8388608
  23.3 4.8 %collective-permute-start = (bf16[2,512,2048]{1,2,0:T(8,128)(2,1)}, bf16[2,512,2048]{1,2,0:T(8,128)(2,1)}, u32[]{:S(2)}, u32[]{:S(2)}) collective-permute-start(bf16[2,512,2048]{1,2,0:T(8,128)(2,1)} %copy.24), channel_id=1, source_target_pairs={{0,1},{1,2},{2,3},{3,4},{4,5},{5,6},{6,7},{7,8},{8,9},{9,10},{10,1... | collective-permute-start | bytes 12582920 | tf_op jit(solution)/shard_map/ppermute | solution.py:18
  33.2 40.7 %collective-permute-done = bf16[2,512,2048]{1,2,0:T(8,128)(2,1)} collective-permute-done((bf16[2,512,2048]{1,2,0:T(8,128)(2,1)}, bf16[2,512,2048]{1,2,0:T(8,128)(2,1)}, u32[]{:S(2)}, u32[]{:S(2)}) %collective-permute-start) | collective-permute-done | bytes 4194336 | tf_op jit(solution)/shard_map/ppermute | solution.py:18
  73.9 6.9 %collective-permute-done.1 = bf16[2,512,2048]{1,2,0:T(8,128)(2,1)} collective-permute-done((bf16[2,512,2048]{1,2,0:T(8,128)(2,1)}, bf16[2,512,2048]{1,2,0:T(8,128)(2,1)}, u32[]{:S(2)}, u32[]{:S(2)}) %collective-permute-start.1) | collective-permute-done | bytes 4194336 | tf_op jit(solution)/shard_map/ppermute | solution.py:20
  80.7 10.3 %pad_maximum_fusion = bf16[2,1536,2048]{1,2,0:T(8,128)(2,1)} fusion(bf16[2,512,2048]{1,2,0:T(8,128)(2,1)} %collective-permute-done.1, bf16[2,512,2048]{1,2,0:T(8,128)(2,1)} %copy.24, bf16[2,512,2048]{1,2,0:T(8,128)(2,1)} %collective-permute-done), kind=kLoop, calls=%fused_computation.20 | loop fusion | flops 37748736 | bytes 25165824 | tf_op jit(solution)/shard_map/concatenate | solution.py:16
  91.0 120.5 %while.13 = (s32[]{:T(128)}, bf16[8,2,512,128]{2,3,0,1:T(8,128)(2,1)}, s32[8]{0:T(128)S(1)}, bf16[2,1536,2048]{1,2,0:T(8,128)(2,1)}, bf16[2,512,1024]{2,1,0:T(8,...) while((s32[]{:T(128)}, ...), condition=%wide.region_4.5_spmd.clone, body=%wide.region_1.4_spmd.clone.sunk | while | flops 844099584 | bytes 47763212 | solution.py:77
  98.5 3.5 fusion.47
  102.0 3.3 fusion.48
  113.5 3.5 fusion.47
  117.0 3.3 fusion.48
  128.6 3.5 fusion.47
  132.1 3.3 fusion.48
  143.6 3.5 fusion.47
  147.2 3.3 fusion.48
  158.7 3.5 fusion.47
  173.8 3.5 fusion.47
  177.3 3.3 fusion.48
  188.8 3.5 fusion.47
  203.9 3.5 fusion.47
  213.3 101.7 %all_to_all.10 = bf16[2,512,32,32]{1,3,0,2:T(8,128)(2,1)} all-to-all(bf16[2,512,32,32]{1,3,0,2:T(8,128)(2,1)S(1)} %copy.18), channel_id=1, replica_groups=mesh['dp'=8,'seq'=32] {'seq'}, dimensions={2} | all-to-all | bytes 4194304 | tf_op jit(solution)/shard_map/all_to_all | solution.py:100
  318.3 5.7 %all-to-all-start.1 = ((bf16[2,512,32,32]{1,3,0,2:T(8,128)(2,1)}), bf16[2,512,32,32]{1,3,0,2:T(8,128)(2,1)}, u32[]{:S(2)}, u32[]{:S(2)}) async-start(bf16[2,512,32,32]{1,3,0,2:T(8,128)(2,1)} %rev.6), calls=%async_computation.1 | async-start | bytes 4194304 | tf_op jit(solution)/shard_map/all_to_all | solution.py:101
  327.3 47.0 %all-to-all-done.1 = bf16[2,512,32,32]{1,3,0,2:T(8,128)(2,1)} async-done(((bf16[2,512,32,32]{1,3,0,2:T(8,128)(2,1)}), bf16[2,512,32,32]{1,3,0,2:T(8,128)(2,1)}, u32[]{:S(2)}, u32[]{:S(2)}) %all-to-all-start.1) | async-done | bytes 2097184 | tf_op jit(solution)/shard_map/all_to_all | solution.py:101
  377.4 27.7 %rev.7 = bf16[2,512,1024]{1,2,0:T(8,128)(2,1)S(1)} reverse(bf16[2,512,1024]{1,2,0:T(8,128)(2,1)} %bitcast.65), dimensions={1,2} | reverse | bytes 4194304 | tf_op jit(solution)/shard_map/rev | solution.py:90
  (101 shorter events, 101.8 us)
Async XLA Ops:
  0.6 2.0 copy-start.5
  0.6 2.2 copy-start.4
  0.7 2.7 copy-start.6
  0.7 3.5 slice-start
  2.8 2.1 slice-start.1
  12.0 2.7 copy-start.3
  23.3 50.6 %collective-permute-start = (bf16[2,512,2048]{1,2,0:T(8,128)(2,1)}, bf16[2,512,2048]{1,2,0:T(8,128)(2,1)}, u32[]{:S(2)}, u32[]{:S(2)}) collective-permute-start(bf16[2,512,2048]{1,2,0:T(8,128)(2,1)} %copy.24), channel_id=1, source_target_pairs={{0,1},{1,2},{2,3},{3,4},{4,5},{5,6},{6,7},{7,8},{8,9},{9,10},{10,1... | collective-permute-start | bytes 12582920 | tf_op jit(solution)/shard_map/ppermute | solution.py:18
  28.1 52.6 %collective-permute-start.1 = (bf16[2,512,2048]{1,2,0:T(8,128)(2,1)}, bf16[2,512,2048]{1,2,0:T(8,128)(2,1)}, u32[]{:S(2)}, u32[]{:S(2)}) collective-permute-start(bf16[2,512,2048]{1,2,0:T(8,128)(2,1)} %copy.24), channel_id=1, source_target_pairs={{1,0},{2,1},{3,2},{4,3},{5,4},{6,5},{7,6},{8,7},{9,8},{10,9},{11,1... | collective-permute-start | bytes 12582920 | tf_op jit(solution)/shard_map/ppermute | solution.py:20
  315.0 9.0 %copy-start = (bf16[8,2,512,128]{2,3,0,1:T(8,128)(2,1)S(1)}, bf16[8,2,512,128]{2,3,0,1:T(8,128)(2,1)}, u32[]{:S(2)}) copy-start(bf16[8,2,512,128]{2,3,0,1:T(8,128)(2,1)} %get-tuple-element.79) | copy-start | bytes 6291460
  318.3 56.0 %all-to-all-start.1 = ((bf16[2,512,32,32]{1,3,0,2:T(8,128)(2,1)}), bf16[2,512,32,32]{1,3,0,2:T(8,128)(2,1)}, u32[]{:S(2)}, u32[]{:S(2)}) async-start(bf16[2,512,32,32]{1,3,0,2:T(8,128)(2,1)} %rev.6), calls=%async_computation.1 | async-start | bytes 4194304 | tf_op jit(solution)/shard_map/all_to_all | solution.py:101
  405.1 1.6 copy-start.1
  405.1 2.2 copy-start.2
where the time goes:
time: 415 us; the launch traced here: 411 us
  blocking collectives  102 us (25%)
  waiting for transfers between devices  94.5 us (23%)
  local copies, waits for them, and re-layouts  89.9 us (22%)
  matrix products  53.6 us (13%)
  other arithmetic  52.5 us (13%)
  starting transfers between devices  12.4 us (3%)
  loops' own time  5.67 us (1%)
    all_to_all x1, blocking collectives, per_device(): lax.all_to_all(pieces, 'seq', split_axis=2, concat_axis=2, tiled=True)  102 us
    all_to_all x1, waiting for transfers between devices, per_device(): lax.all_to_all(spread, 'seq', split_axis=2, concat_axis=2, tiled=True)  47 us
    ppermute x1, waiting for transfers between devices, extended_2(): lax.ppermute(tail, axis, [(i, (i + 1) % count) for i in range(ends)])  40.7 us
    reduce_sum x8, other arithmetic, group_heads(): denom = jnp.sum(probs, axis=-1)  28.1 us
    rev x1, local copies, waits for them, and re-layouts, combine_outputs(): partner = moved[:, ::-1, ::-1].astype(jnp.float32)  27.7 us
    dot_general x8, matrix products, group_heads(): jnp.einsum('shrk,skhd->srhd', weights, vgroup, preferred_element_type=jnp...  26.5 us
    dot_general x8, matrix products, group_heads(): jnp.einsum('srhd,skhd->shrk', qgroup, kgroup, preferred_element_type=jnp....  20 us
    unnamed x22, local copies, waits for them, and re-layouts  14.5 us
  transfers between devices with their start and end apart: 3, of which 3 were waited for; matrix products, arithmetic and copies ran while one was open for 2% of the time, Pallas kernels for 0%

commit v1 on v0

v1 whole, which is shorter than its diff:
```python
import functools

import jax
import jax.numpy as jnp
from jax import lax
from jax.experimental import pallas as pl
from jax.experimental.pallas import tpu as pltpu
from jax.sharding import PartitionSpec as P

HEADS = 16
WINDOW = 512
LOG2E = 1.4426950408889634
NEG = -1e30
VMEM_LIMIT = 56 * 1024 * 1024


def project_kernel(n_parts, rows, q_blocks, scale, *refs):
    x_refs = refs[:n_parts]
    gain_ref, w_ref, out_ref, hn_ref = refs[n_parts:]
    j = pl.program_id(0)

    @pl.when(j == 0)
    def _():
        g = gain_ref[...].astype(jnp.float32)
        for n, x_ref in enumerate(x_refs):
            xf = x_ref[...].astype(jnp.float32)
            meansq = jnp.mean(xf * xf, axis=-1, keepdims=True)
            hn = xf * lax.rsqrt(meansq + 1e-6) * g
            hn_ref[n * rows : (n + 1) * rows, :] = hn.astype(jnp.bfloat16)

    acc = jnp.dot(hn_ref[...], w_ref[...], preferred_element_type=jnp.float32)
    if q_blocks:
        acc = acc * jnp.where(j < q_blocks, scale, 1.0)
    out_ref[...] = acc.astype(jnp.bfloat16)


def project(xs, gain, w, first, block, scale):
    rows, width = xs[0].shape
    n = len(xs)
    columns = w.shape[1] - first
    off = first // block
    q_blocks = max(0, (width - first) // block)
    return pl.pallas_call(
        functools.partial(project_kernel, n, rows, q_blocks, scale),
        out_shape=jax.ShapeDtypeStruct((n * rows, columns), jnp.bfloat16),
        grid=(columns // block,),
        in_specs=[pl.BlockSpec((rows, width), lambda j: (0, 0))] * n
        + [
            pl.BlockSpec((1, width), lambda j: (0, 0)),
            pl.BlockSpec((width, block), lambda j: (0, off + j)),
        ],
        out_specs=pl.BlockSpec((n * rows, block), lambda j: (0, j)),
        scratch_shapes=[pltpu.VMEM((n * rows, width), jnp.bfloat16)],
        compiler_params=pltpu.CompilerParams(vmem_limit_bytes=VMEM_LIMIT),
        cost_estimate=pl.CostEstimate(
            flops=2 * n * rows * width * columns,
            bytes_accessed=2 * (n * rows * (width + columns) + width * columns),
            transcendentals=0,
        ),
        name="project",
    )(*xs, gain, w)


def exchange_matrix(n):
    r = lax.broadcasted_iota(jnp.int32, (n, n), 0)
    c = lax.broadcasted_iota(jnp.int32, (n, n), 1)
    return (r + c == n - 1).astype(jnp.bfloat16)


def flipped(block):
    rows, columns = block.shape
    half = rows // 2
    t = jnp.dot(block, exchange_matrix(columns), preferred_element_type=jnp.float32)
    t = t.astype(jnp.bfloat16)
    ex = exchange_matrix(half)
    top = jnp.dot(ex, t[half:], preferred_element_type=jnp.float32)
    bottom = jnp.dot(ex, t[:half], preferred_element_type=jnp.float32)
    return jnp.concatenate([top, bottom], axis=0)


def attention_kernel(tile, combine, valid_ref, q_ref, kl_ref, ko_ref, kr_ref, vl_ref, vo_ref, vr_ref, *refs):
    if combine:
        near_ref, out_ref, kbuf, vbuf = refs
    else:
        out_ref, kbuf, vbuf = refs
    rows, width = q_ref.shape
    head = width // 2
    has_left = valid_ref[0] > 0
    has_right = valid_ref[1] > 0
    kbuf[:rows] = jnp.where(has_left, kl_ref[...], ko_ref[...])
    kbuf[rows : 2 * rows] = ko_ref[...]
    kbuf[2 * rows :] = jnp.where(has_right, kr_ref[...], ko_ref[...])
    ones = jnp.ones((rows, width), jnp.bfloat16)
    none = jnp.zeros((rows, width), jnp.bfloat16)
    vbuf[:rows, :width] = jnp.where(has_left, vl_ref[...], none)
    vbuf[:rows, width:] = jnp.where(has_left, ones, none)
    vbuf[rows : 2 * rows, :width] = vo_ref[...]
    vbuf[rows : 2 * rows, width:] = ones
    vbuf[2 * rows :, :width] = jnp.where(has_right, vr_ref[...], none)
    vbuf[2 * rows :, width:] = jnp.where(has_right, ones, none)

    span = tile + 2 * WINDOW
    r = lax.broadcasted_iota(jnp.int32, (tile, tile), 0)
    c = lax.broadcasted_iota(jnp.int32, (tile, tile), 1)
    low = c >= r
    high = c <= r
    lane = lax.broadcasted_iota(jnp.int32, (tile, width), 1)
    pieces = []
    for t in range(rows // tile):
        q = q_ref[t * tile : (t + 1) * tile, :]
        keys = kbuf[t * tile : t * tile + span, :]
        values = vbuf[t * tile : t * tile + span, :]
        outs = []
        for h in range(2):
            mine = (lane < head) if h == 0 else (lane >= head)
            qh = jnp.where(mine, q, jnp.zeros_like(q))
            s = lax.dot_general(
                qh, keys, (((1,), (1,)), ((), ())), preferred_element_type=jnp.float32
            )
            s_low = jnp.where(low, s[:, :tile], NEG)
            s_mid = s[:, tile : 2 * WINDOW]
            s_high = jnp.where(high, s[:, 2 * WINDOW :], NEG)
            s = jnp.concatenate([s_low, s_mid, s_high], axis=1)
            top = jnp.max(s, axis=-1, keepdims=True)
            p = jnp.exp2(s - top).astype(jnp.bfloat16)
            o = jnp.dot(p, values, preferred_element_type=jnp.float32)
            outs.append(o[:, :width] / o[:, width:])
        pieces.append(jnp.where(lane < head, outs[0], outs[1]).astype(jnp.bfloat16))
    a = jnp.concatenate(pieces, axis=0)
    if combine:
        out_ref[...] = (near_ref[...].astype(jnp.float32) + flipped(a)).astype(jnp.bfloat16)
    else:
        out_ref[...] = a


def attention(own, halo, valid, first, count, near=None):
    rows = own.shape[0]
    width = own.shape[1] // 3
    pw = 2 * (width // HEADS)
    n = width // pw
    f = first

    def spec(row, col):
        return pl.BlockSpec((rows, pw), lambda g: (row, col + f + g))

    operands = [valid, own, halo, own, halo, halo, own, halo]
    in_specs = [
        pl.BlockSpec(memory_space=pltpu.SMEM),
        spec(0, 0),
        spec(0, 0),
        spec(0, n),
        spec(1, 0),
        spec(0, n),
        spec(0, 2 * n),
        spec(1, n),
    ]
    if near is None:
        out_spec = pl.BlockSpec((rows, pw), lambda g: (0, g))
    else:
        operands.append(near)
        in_specs.append(pl.BlockSpec((rows, pw), lambda g: (0, n - 1 - f - g)))
        out_spec = pl.BlockSpec((rows, pw), lambda g: (0, count - 1 - g))
    return pl.pallas_call(
        functools.partial(attention_kernel, min(256, rows), near is not None),
        out_shape=jax.ShapeDtypeStruct((rows, count * pw), jnp.bfloat16),
        grid=(count,),
        in_specs=in_specs,
        out_specs=out_spec,
        scratch_shapes=[
            pltpu.VMEM((rows + 2 * WINDOW, pw), jnp.bfloat16),
            pltpu.VMEM((rows + 2 * WINDOW, 2 * pw), jnp.bfloat16),
        ],
        compiler_params=pltpu.CompilerParams(vmem_limit_bytes=VMEM_LIMIT),
        cost_estimate=pl.CostEstimate(
            flops=16 * count * rows * (256 + 2 * WINDOW) * 2 * pw,
            bytes_accessed=16 * count * rows * pw,
            transcendentals=2 * count * rows * (256 + 2 * WINDOW),
        ),
        name="attention",
    )(*operands)


def finish_kernel(n, *refs):
    mine, moved, (fwd_ref, rev_ref) = refs[:n], refs[n : 2 * n], refs[2 * n :]
    width = mine[0].shape[1]
    for k in range(n):
        fwd_ref[:, (n - 1 - k) * width : (n - k) * width] = mine[k][...]
        rev_ref[:, k * width : (k + 1) * width] = flipped(moved[k][...]).astype(jnp.bfloat16)


def finish(mine, moved):
    rows = mine[0].shape[0]
    n = len(mine)
    width = sum(m.shape[1] for m in mine)
    out = jax.ShapeDtypeStruct((rows, width), jnp.bfloat16)
    return pl.pallas_call(
        functools.partial(finish_kernel, n),
        out_shape=(out, out),
        compiler_params=pltpu.CompilerParams(vmem_limit_bytes=VMEM_LIMIT),
        cost_estimate=pl.CostEstimate(
            flops=2 * rows * width * 512, bytes_accessed=8 * rows * width, transcendentals=0
        ),
        name="finish",
    )(*mine, *moved)


def per_device(x_fwd, x_rev, gain, w_qkv):
    count = lax.axis_size("seq")
    index = lax.axis_index("seq")
    width = x_fwd.shape[1]
    scale = (width // HEADS) ** (-0.5) * LOG2E
    gain = gain.reshape(1, width)
    mirror = [(i, count - 1 - i) for i in range(count)]
    up = [(i, i + 1) for i in range(count - 1)]
    down = [(i + 1, i) for i in range(count - 1)]

    has_prev = (index > 0).astype(jnp.int32)
    has_next = (index < count - 1).astype(jnp.int32)
    valid_f = jnp.stack([has_prev, has_next])
    valid_r = jnp.stack([has_next, has_prev])

    r_own = lax.ppermute(x_rev, "seq", mirror)
    f_left = lax.ppermute(x_fwd, "seq", up)
    f_right = lax.ppermute(x_fwd, "seq", down)
    r_left = lax.ppermute(r_own, "seq", down)
    r_right = lax.ppermute(r_own, "seq", up)

    pairs = HEADS // 2
    f_qkv = project([x_fwd], gain, w_qkv, 0, 512, scale)
    f_halo = project([f_left, f_right], gain, w_qkv, width, 512, scale)
    a_f = attention(f_qkv, f_halo, valid_f, 0, pairs)

    r_qkv = project([r_own], gain, w_qkv, 0, 512, scale)
    r_halo = project([r_left, r_right], gain, w_qkv, width, 512, scale)
    steps = 4
    each = pairs // steps
    mine, moved = [], []
    for k in range(steps):
        if k >= 2:
            moved[k - 2], r_qkv = lax.optimization_barrier((moved[k - 2], r_qkv))
        y = attention(r_qkv, r_halo, valid_r, k * each, each, near=a_f)
        mine.append(y)
        moved.append(lax.ppermute(y, "seq", mirror))
    return finish(mine, moved)


def solution(mesh):
    in_specs = (P(("dp", "seq"), None), P(("dp", "seq"), None), P(), P())
    out_specs = (P(("dp", "seq"), None), P(("dp", "seq"), None))
    return jax.shard_map(
        per_device, mesh=mesh, in_specs=in_specs, out_specs=out_specs, check_vma=False
    )
```

time: 415 us -> 189 us (0.46)
  the two profiles are of different devices: /device:TPU:25 before, /device:TPU:1 now
where the time goes in v1:
time: 189 us; the launch traced here: 188 us
  Pallas kernels  86.8 us (46%)
  waiting for transfers between devices  56.1 us (30%)
  starting transfers between devices  37.6 us (20%)
  local copies, waits for them, and re-layouts  5.92 us (3%)
    pallas_call x5, Pallas kernels, attention(): pl.pallas_call(functools.partial(attention_kernel, min(256, rows), near i...  47.3 us
    pallas_call x4, Pallas kernels, project(): pl.pallas_call(functools.partial(project_kernel, n, rows, q_blocks, scale...  35.7 us
    ppermute x1, waiting for transfers between devices, per_device(): r_own = lax.ppermute(x_rev, 'seq', mirror)  30.7 us
    ppermute x4, waiting for transfers between devices, per_device(): moved.append(lax.ppermute(y, 'seq', mirror))  25.3 us
    ppermute x4, starting transfers between devices, per_device(): moved.append(lax.ppermute(y, 'seq', mirror))  10.8 us
    ppermute x1, starting transfers between devices, per_device(): r_right = lax.ppermute(r_own, 'seq', up)  10.4 us
    ppermute x1, starting transfers between devices, per_device(): r_own = lax.ppermute(x_rev, 'seq', mirror)  9.68 us
    unnamed x20, local copies, waits for them, and re-layouts  4.64 us
  transfers between devices with their start and end apart: 9, of which 4 were waited for; matrix products, arithmetic and copies ran while one was open for 1% of the time, Pallas kernels for 32%

profile of v1, /device:TPU:1, one launch (start us, length us, event | category | flops | bytes accessed | tf_op | source)
XLA Modules:
  0.0 187.8 jit_solution(1493712571209864468)
XLA Ops:
  0.6 9.7 %collective-permute-start = (bf16[512,1024]{1,0:T(8,128)(2,1)}, bf16[512,1024]{1,0:T(8,128)(2,1)S(1)}, u32[]{:S(2)}, u32[]{:S(2)}) collective-permute-start(bf16[512,1024]{1,0:T(8,128)(2,1)} %param.5), channel_id=1, source_target_pairs={{0,31},{1,30},{2,29},{3,28},{4,27},{5,26},{6,25},{7,24},{8,23},{9,... | collective-permute-start | bytes 3145736 | tf_op jit(solution)/shard_map/ppermute | solution.py:222
  10.3 1.9 %collective-permute-start.3 = (bf16[512,1024]{1,0:T(8,128)(2,1)}, bf16[512,1024]{1,0:T(8,128)(2,1)S(1)}, u32[]{:S(2)}, u32[]{:S(2)}) collective-permute-start(bf16[512,1024]{1,0:T(8,128)(2,1)} %refs_0_.1), channel_id=1, source_target_pairs={{0,1},{1,2},{2,3},{3,4},{4,5},{5,6},{6,7},{7,8},{8,9},{9,10},{10,1... | collective-permute-start | bytes 3145736 | tf_op jit(solution)/shard_map/ppermute | solution.py:223
  12.2 2.5 %collective-permute-start.4 = (bf16[512,1024]{1,0:T(8,128)(2,1)}, bf16[512,1024]{1,0:T(8,128)(2,1)S(1)}, u32[]{:S(2)}, u32[]{:S(2)}) collective-permute-start(bf16[512,1024]{1,0:T(8,128)(2,1)} %refs_0_.1), channel_id=1, source_target_pairs={{1,0},{2,1},{3,2},{4,3},{5,4},{6,5},{7,6},{8,7},{9,8},{10,9},{11,1... | collective-permute-start | bytes 3145736 | tf_op jit(solution)/shard_map/ppermute | solution.py:224
  14.7 1.3 reshape.7.refs_1_.refs_2_
  16.6 8.7 %project.6.q_ref.ko_ref.vo_ref = bf16[512,3072]{1,0:T(8,128)(2,1)} custom-call(bf16[512,1024]{1,0:T(8,128)(2,1)} %refs_0_.1, bf16[1,1024]{1,0:T(2,128)(2,1)} %reshape.7.refs_1_.refs_2_, bf16[1024,3072]{1,0:T(8,128)(2,1)} %refs_3_.3), custom_call_target="tpu_custom_call" | custom-call | flops 3221225472 | bytes 10485760 | tf_op jit(solution)/shard_map/project/pallas_call | solution.py:43
  25.3 30.7 %collective-permute-done.refs_0_ = bf16[512,1024]{1,0:T(8,128)(2,1)S(1)} collective-permute-done((bf16[512,1024]{1,0:T(8,128)(2,1)}, bf16[512,1024]{1,0:T(8,128)(2,1)S(1)}, u32[]{:S(2)}, u32[]{:S(2)}) %collective-permute-start) | collective-permute-done | bytes 1048608 | tf_op jit(solution)/shard_map/ppermute | solution.py:222
  56.1 2.3 %collective-permute-start.1 = (bf16[512,1024]{1,0:T(8,128)(2,1)S(1)}, bf16[512,1024]{1,0:T(8,128)(2,1)S(1)}, u32[]{:S(2)}, u32[]{:S(2)}) collective-permute-start(bf16[512,1024]{1,0:T(8,128)(2,1)S(1)} %collective-permute-done.refs_0_), channel_id=1, source_target_pairs={{1,0},{2,1},{3,2},{4,3},{5,4},{6,5},{7,6},{8,7},{9,8},{10,9},{11,1... | collective-permute-start | bytes 3145736 | tf_op jit(solution)/shard_map/ppermute | solution.py:225
  58.4 10.4 %collective-permute-start.2 = (bf16[512,1024]{1,0:T(8,128)(2,1)S(1)}, bf16[512,1024]{1,0:T(8,128)(2,1)S(1)}, u32[]{:S(2)}, u32[]{:S(2)}) collective-permute-start(bf16[512,1024]{1,0:T(8,128)(2,1)S(1)} %collective-permute-done.refs_0_), channel_id=1, source_target_pairs={{0,1},{1,2},{2,3},{3,4},{4,5},{5,6},{6,7},{7,8},{8,9},{9,10},{10,1... | collective-permute-start | bytes 3145736 | tf_op jit(solution)/shard_map/ppermute | solution.py:226
  69.8 1.0 copy-done.7
  70.9 9.2 %project.7.kl_ref.kr_ref.vl_ref.vr_ref = bf16[1024,2048]{1,0:T(8,128)(2,1)} custom-call(bf16[512,1024]{1,0:T(8,128)(2,1)} %copy-done.6, bf16[512,1024]{1,0:T(8,128)(2,1)} %copy-done.7, bf16[1,1024]{1,0:T(2,128)(2,1)} %reshape.7.refs_1_.refs_2_, bf16[1024,3072]{1,0:T(8,128)(2,1)} %refs_3_.3), custom_call_target="tpu_custom_call" | custom-call | flops 4294967296 | bytes 10485760 | tf_op jit(solution)/shard_map/project/pallas_call | solution.py:43
  80.0 19.2 %attention.5.refs_0_ = bf16[512,1024]{1,0:T(8,128)(2,1)} custom-call(s32[2]{0:T(128)} %get-tuple-element.11.valid_ref, bf16[512,3072]{1,0:T(8,128)(2,1)} %project.6.q_ref.ko_ref.vo_ref, bf16[1024,2048]{1,0:T(8,128)(2,1)} %project.7.kl_ref.kr_ref.vl_ref.vr_ref, bf16[512,3072]{1,0:T(8,128)(2,1)} %project.6.q_ref.ko_ref.vo_ref, ...), custom_call_target="tpu_custom_call" | custom-call | flops 21474836480 | bytes 8388608 | tf_op jit(solution)/shard_map/attention/pallas_call | solution.py:163
  99.3 8.7 %project.4.q_ref.ko_ref.vo_ref = bf16[512,3072]{1,0:T(8,128)(2,1)} custom-call(bf16[512,1024]{1,0:T(8,128)(2,1)} %copy-done.5, bf16[1,1024]{1,0:T(2,128)(2,1)} %reshape.7.refs_1_.refs_2_, bf16[1024,3072]{1,0:T(8,128)(2,1)} %refs_3_.3), custom_call_target="tpu_custom_call" | custom-call | flops 3221225472 | bytes 10485760 | tf_op jit(solution)/shard_map/project/pallas_call | solution.py:43
  108.9 1.0 copy-done.9
  109.9 9.2 %project.5.kl_ref.kr_ref.vl_ref.vr_ref = bf16[1024,2048]{1,0:T(8,128)(2,1)} custom-call(bf16[512,1024]{1,0:T(8,128)(2,1)} %copy-done.8, bf16[512,1024]{1,0:T(8,128)(2,1)} %copy-done.9, bf16[1,1024]{1,0:T(2,128)(2,1)} %reshape.7.refs_1_.refs_2_, bf16[1024,3072]{1,0:T(8,128)(2,1)} %refs_3_.3), custom_call_target="tpu_custom_call" | custom-call | flops 4294967296 | bytes 10485760 | tf_op jit(solution)/shard_map/project/pallas_call | solution.py:43
  119.1 7.0 %attention.6.refs_0_ = bf16[512,256]{1,0:T(8,128)(2,1)} custom-call(s32[2]{0:T(128)} %get-tuple-element.10.valid_ref, bf16[512,3072]{1,0:T(8,128)(2,1)} %project.4.q_ref.ko_ref.vo_ref, bf16[1024,2048]{1,0:T(8,128)(2,1)} %project.5.kl_ref.kr_ref.vl_ref.vr_ref, bf16[512,3072]{1,0:T(8,128)(2,1)} %project.4.q_ref.ko_ref.vo_ref, ...), custom_call_target="tpu_custom_call" | custom-call | flops 5368709120 | bytes 2097152 | tf_op jit(solution)/shard_map/attention/pallas_call | solution.py:163
  126.0 7.0 %attention.7.refs_1_ = bf16[512,256]{1,0:T(8,128)(2,1)} custom-call(s32[2]{0:T(128)} %get-tuple-element.10.valid_ref, bf16[512,3072]{1,0:T(8,128)(2,1)} %project.4.q_ref.ko_ref.vo_ref, bf16[1024,2048]{1,0:T(8,128)(2,1)} %project.5.kl_ref.kr_ref.vl_ref.vr_ref, bf16[512,3072]{1,0:T(8,128)(2,1)} %project.4.q_ref.ko_ref.vo_ref, ...), custom_call_target="tpu_custom_call" | custom-call | flops 5368709120 | bytes 2097152 | tf_op jit(solution)/shard_map/attention/pallas_call | solution.py:163
  133.0 5.3 %collective-permute-start.6 = (bf16[512,256]{1,0:T(8,128)(2,1)}, bf16[512,256]{1,0:T(8,128)(2,1)S(1)}, u32[]{:S(2)}, u32[]{:S(2)}) collective-permute-start(bf16[512,256]{1,0:T(8,128)(2,1)} %attention.7.refs_1_), channel_id=1, source_target_pairs={{0,31},{1,30},{2,29},{3,28},{4,27},{5,26},{6,25},{7,24},{8,23},{9,... | collective-permute-start | bytes 786440 | tf_op jit(solution)/shard_map/ppermute | solution.py:243
  138.4 11.0 %collective-permute-done.5.refs_4_ = bf16[512,256]{1,0:T(8,128)(2,1)S(1)} collective-permute-done((bf16[512,256]{1,0:T(8,128)(2,1)}, bf16[512,256]{1,0:T(8,128)(2,1)S(1)}, u32[]{:S(2)}, u32[]{:S(2)}) %collective-permute-start.5) | collective-permute-done | bytes 262176 | tf_op jit(solution)/shard_map/ppermute | solution.py:243
  149.3 7.0 %attention.8.refs_2_ = bf16[512,256]{1,0:T(8,128)(2,1)} custom-call(s32[2]{0:T(128)} %get-tuple-element.10.valid_ref, bf16[512,3072]{1,0:T(8,128)(2,1)} %project.4.q_ref.ko_ref.vo_ref, bf16[1024,2048]{1,0:T(8,128)(2,1)} %project.5.kl_ref.kr_ref.vl_ref.vr_ref, bf16[512,3072]{1,0:T(8,128)(2,1)} %project.4.q_ref.ko_ref.vo_ref, ...), custom_call_target="tpu_custom_call" | custom-call | flops 5368709120 | bytes 2097152 | tf_op jit(solution)/shard_map/attention/pallas_call | solution.py:163
  156.4 7.1 %attention.9.refs_3_ = bf16[512,256]{1,0:T(8,128)(2,1)} custom-call(s32[2]{0:T(128)} %get-tuple-element.10.valid_ref, bf16[512,3072]{1,0:T(8,128)(2,1)} %project.4.q_ref.ko_ref.vo_ref, bf16[1024,2048]{1,0:T(8,128)(2,1)} %project.5.kl_ref.kr_ref.vl_ref.vr_ref, bf16[512,3072]{1,0:T(8,128)(2,1)} %project.4.q_ref.ko_ref.vo_ref, ...), custom_call_target="tpu_custom_call" | custom-call | flops 5368709120 | bytes 2097152 | tf_op jit(solution)/shard_map/attention/pallas_call | solution.py:163
  163.6 5.3 %collective-permute-start.7 = (bf16[512,256]{1,0:T(8,128)(2,1)S(1)}, bf16[512,256]{1,0:T(8,128)(2,1)S(1)}, u32[]{:S(2)}, u32[]{:S(2)}) collective-permute-start(bf16[512,256]{1,0:T(8,128)(2,1)S(1)} %copy-done), channel_id=1, source_target_pairs={{0,31},{1,30},{2,29},{3,28},{4,27},{5,26},{6,25},{7,24},{8,23},{9,... | collective-permute-start | bytes 786440 | tf_op jit(solution)/shard_map/ppermute | solution.py:243
  168.9 8.9 %collective-permute-done.8.refs_7_ = bf16[512,256]{1,0:T(8,128)(2,1)S(1)} collective-permute-done((bf16[512,256]{1,0:T(8,128)(2,1)}, bf16[512,256]{1,0:T(8,128)(2,1)S(1)}, u32[]{:S(2)}, u32[]{:S(2)}) %collective-permute-start.8) | collective-permute-done | bytes 262176 | tf_op jit(solution)/shard_map/ppermute | solution.py:243
  177.9 5.4 %collective-permute-done.7.refs_6_ = bf16[512,256]{1,0:T(8,128)(2,1)S(1)} collective-permute-done((bf16[512,256]{1,0:T(8,128)(2,1)S(1)}, bf16[512,256]{1,0:T(8,128)(2,1)S(1)}, u32[]{:S(2)}, u32[]{:S(2)}) %collective-permute-start.7) | collective-permute-done | bytes 262176 | tf_op jit(solution)/shard_map/ppermute | solution.py:243
  184.0 3.8 %finish.1 = (bf16[512,1024]{1,0:T(8,128)(2,1)}, bf16[512,1024]{1,0:T(8,128)(2,1)}) custom-call(bf16[512,256]{1,0:T(8,128)(2,1)} %attention.6.refs_0_, bf16[512,256]{1,0:T(8,128)(2,1)} %attention.7.refs_1_, bf16[512,256]{1,0:T(8,128)(2,1)} %attention.8.refs_2_, bf16[512,256]{1,0:T(8,128)(2,1)} %attention.9.refs_3_, bf16[512,256]{1,0:T(8,128)(2,1)} %copy-done.1, ...), custom_call_target="tpu_custom_call" | custom-call | flops 536870912 | bytes 4194304 | tf_op jit(solution)/shard_map/finish/pallas_call | solution.py:196
  (26 shorter events, 3.4 us)
Async XLA Ops:
  0.6 55.4 %collective-permute-start = (bf16[512,1024]{1,0:T(8,128)(2,1)}, bf16[512,1024]{1,0:T(8,128)(2,1)S(1)}, u32[]{:S(2)}, u32[]{:S(2)}) collective-permute-start(bf16[512,1024]{1,0:T(8,128)(2,1)} %param.5), channel_id=1, source_target_pairs={{0,31},{1,30},{2,29},{3,28},{4,27},{5,26},{6,25},{7,24},{8,23},{9,... | collective-permute-start | bytes 3145736 | tf_op jit(solution)/shard_map/ppermute | solution.py:222
  10.3 58.5 %collective-permute-start.3 = (bf16[512,1024]{1,0:T(8,128)(2,1)}, bf16[512,1024]{1,0:T(8,128)(2,1)S(1)}, u32[]{:S(2)}, u32[]{:S(2)}) collective-permute-start(bf16[512,1024]{1,0:T(8,128)(2,1)} %refs_0_.1), channel_id=1, source_target_pairs={{0,1},{1,2},{2,3},{3,4},{4,5},{5,6},{6,7},{7,8},{8,9},{9,10},{10,1... | collective-permute-start | bytes 3145736 | tf_op jit(solution)/shard_map/ppermute | solution.py:223
  12.2 56.6 %collective-permute-start.4 = (bf16[512,1024]{1,0:T(8,128)(2,1)}, bf16[512,1024]{1,0:T(8,128)(2,1)S(1)}, u32[]{:S(2)}, u32[]{:S(2)}) collective-permute-start(bf16[512,1024]{1,0:T(8,128)(2,1)} %refs_0_.1), channel_id=1, source_target_pairs={{1,0},{2,1},{3,2},{4,3},{5,4},{6,5},{7,6},{8,7},{9,8},{10,9},{11,1... | collective-permute-start | bytes 3145736 | tf_op jit(solution)/shard_map/ppermute | solution.py:224
  56.1 24.0 %copy-start.5 = (bf16[512,1024]{1,0:T(8,128)(2,1)}, bf16[512,1024]{1,0:T(8,128)(2,1)S(1)}, u32[]{:S(2)}) copy-start(bf16[512,1024]{1,0:T(8,128)(2,1)S(1)} %collective-permute-done.refs_0_) | copy-start | bytes 3145732
  56.1 51.9 %collective-permute-start.1 = (bf16[512,1024]{1,0:T(8,128)(2,1)S(1)}, bf16[512,1024]{1,0:T(8,128)(2,1)S(1)}, u32[]{:S(2)}, u32[]{:S(2)}) collective-permute-start(bf16[512,1024]{1,0:T(8,128)(2,1)S(1)} %collective-permute-done.refs_0_), channel_id=1, source_target_pairs={{1,0},{2,1},{3,2},{4,3},{5,4},{6,5},{7,6},{8,7},{9,8},{10,9},{11,1... | collective-permute-start | bytes 3145736 | tf_op jit(solution)/shard_map/ppermute | solution.py:225
  58.4 49.6 %collective-permute-start.2 = (bf16[512,1024]{1,0:T(8,128)(2,1)S(1)}, bf16[512,1024]{1,0:T(8,128)(2,1)S(1)}, u32[]{:S(2)}, u32[]{:S(2)}) collective-permute-start(bf16[512,1024]{1,0:T(8,128)(2,1)S(1)} %collective-permute-done.refs_0_), channel_id=1, source_target_pairs={{0,1},{1,2},{2,3},{3,4},{4,5},{5,6},{6,7},{7,8},{8,9},{9,10},{10,1... | collective-permute-start | bytes 3145736 | tf_op jit(solution)/shard_map/ppermute | solution.py:226
  68.8 1.0 copy-start.6
  69.8 1.0 copy-start.7
  108.0 1.0 copy-start.8
  108.9 1.0 copy-start.9
  126.0 23.3 %collective-permute-start.5 = (bf16[512,256]{1,0:T(8,128)(2,1)}, bf16[512,256]{1,0:T(8,128)(2,1)S(1)}, u32[]{:S(2)}, u32[]{:S(2)}) collective-permute-start(bf16[512,256]{1,0:T(8,128)(2,1)} %attention.6.refs_0_), channel_id=1, source_target_pairs={{0,31},{1,30},{2,29},{3,28},{4,27},{5,26},{6,25},{7,24},{8,23},{9,... | collective-permute-start | bytes 786440 | tf_op jit(solution)/shard_map/ppermute | solution.py:243
  133.0 23.4 %collective-permute-start.6 = (bf16[512,256]{1,0:T(8,128)(2,1)}, bf16[512,256]{1,0:T(8,128)(2,1)S(1)}, u32[]{:S(2)}, u32[]{:S(2)}) collective-permute-start(bf16[512,256]{1,0:T(8,128)(2,1)} %attention.7.refs_1_), channel_id=1, source_target_pairs={{0,31},{1,30},{2,29},{3,28},{4,27},{5,26},{6,25},{7,24},{8,23},{9,... | collective-permute-start | bytes 786440 | tf_op jit(solution)/shard_map/ppermute | solution.py:243
  149.3 7.1 %copy-start.1 = (bf16[512,256]{1,0:T(8,128)(2,1)}, bf16[512,256]{1,0:T(8,128)(2,1)S(1)}, u32[]{:S(2)}) copy-start(bf16[512,256]{1,0:T(8,128)(2,1)S(1)} %collective-permute-done.5.refs_4_) | copy-start | bytes 786436
  156.4 7.2 %copy-start = (bf16[512,256]{1,0:T(8,128)(2,1)S(1)}, bf16[512,256]{1,0:T(8,128)(2,1)}, u32[]{:S(2)}) copy-start(bf16[512,256]{1,0:T(8,128)(2,1)} %attention.8.refs_2_) | copy-start | bytes 786436
  156.4 7.1 %copy-start.2 = (bf16[512,256]{1,0:T(8,128)(2,1)}, bf16[512,256]{1,0:T(8,128)(2,1)S(1)}, u32[]{:S(2)}) copy-start(bf16[512,256]{1,0:T(8,128)(2,1)S(1)} %collective-permute-done.6.refs_5_) | copy-start | bytes 786436
  163.5 14.4 %collective-permute-start.8 = (bf16[512,256]{1,0:T(8,128)(2,1)}, bf16[512,256]{1,0:T(8,128)(2,1)S(1)}, u32[]{:S(2)}, u32[]{:S(2)}) collective-permute-start(bf16[512,256]{1,0:T(8,128)(2,1)} %attention.9.refs_3_), channel_id=1, source_target_pairs={{0,31},{1,30},{2,29},{3,28},{4,27},{5,26},{6,25},{7,24},{8,23},{9,... | collective-permute-start | bytes 786440 | tf_op jit(solution)/shard_map/ppermute | solution.py:243
  163.6 19.7 %collective-permute-start.7 = (bf16[512,256]{1,0:T(8,128)(2,1)S(1)}, bf16[512,256]{1,0:T(8,128)(2,1)S(1)}, u32[]{:S(2)}, u32[]{:S(2)}) collective-permute-start(bf16[512,256]{1,0:T(8,128)(2,1)S(1)} %copy-done), channel_id=1, source_target_pairs={{0,31},{1,30},{2,29},{3,28},{4,27},{5,26},{6,25},{7,24},{8,23},{9,... | collective-permute-start | bytes 786440 | tf_op jit(solution)/shard_map/ppermute | solution.py:243
  177.9 5.4 %copy-start.3 = (bf16[512,256]{1,0:T(8,128)(2,1)}, bf16[512,256]{1,0:T(8,128)(2,1)S(1)}, u32[]{:S(2)}) copy-start(bf16[512,256]{1,0:T(8,128)(2,1)S(1)} %collective-permute-done.8.refs_7_) | copy-start | bytes 786436
  183.3 0.7 copy-start.4
